TPU v7x, 32 devices: a whole 2x2x4 slice. The times are simulated.
32 devices in a mesh: row: 4 (over x, core), col: 8 (over z, y).
Axes of the slice: x: 2, y: 2, z: 4, core: 2. Of those that a mesh axis runs over, the one named last changes fastest.
Arguments:
- green_vectors: float32 [512, 131072], P('row', 'col'), may hold values from -6 to 6
- amplitudes: float32 [2048, 131072], P('row', 'col'), may hold values from -0.015625 to 0.015625
- cholesky: float32 [2048, 4096], P(('row', 'col')), may hold values from -0.125 to 0.125
Outputs:
- force_bias: float32 [512, 4096], P('col', 'row')
All inputs are finite; a program needn't handle non-finite values.
Results may differ from a plain program's by a relative error of at most 0.000084.
Values sent between devices are 32-bit elements; how exact they have to be, the bound alone decides.
A program may use at most 128 MiB of HBM per device.

v0:
```python
import jax
import jax.numpy as jnp
from jax import lax
from jax.sharding import PartitionSpec as P


def per_device(green_vectors, amplitudes, cholesky):
    partial_terms = lax.dot_general(
        lax.all_gather(green_vectors, "row", axis=0, tiled=True),
        amplitudes,
        (((1,), (1,)), ((), ())),
        precision=lax.Precision.HIGHEST,
        preferred_element_type=jnp.float32,
    )
    local_walkers = lax.psum_scatter(partial_terms, "col", scatter_dimension=0, tiled=True)
    row_terms = jnp.dot(
        local_walkers,
        lax.all_gather(cholesky, "col", axis=0, tiled=True),
        precision=lax.Precision.HIGHEST,
        preferred_element_type=jnp.float32,
    )
    return lax.psum_scatter(row_terms, "row", scatter_dimension=1, tiled=True)


def solution(mesh):
    placed = (P("row", "col"), P("row", "col"), P(("row", "col"), None))
    return jax.shard_map(
        per_device, mesh=mesh, in_specs=placed, out_specs=P("col", "row"), check_vma=False
    )
```

profile of v0, /device:TPU:13, one launch (start us, length us, event | category | flops | bytes accessed | tf_op | source)
XLA Modules:
  0.0 443.9 jit_solution(10546769614100060621)
XLA Ops:
  6.5 0.0 all-gather.3.cloned.1.call-start
  6.5 0.7 all-gather.3.cloned.1.call-update
  7.3 0.0 all-gather.5.cloned.1.call-start
  7.3 0.7 all-gather.5.cloned.1.call-update
  8.0 0.0 reduce-scatter.3.cloned.1.call-start
  8.1 203.9 %all-gather.3.cloned.1.call-done = f32[512,16384]{1,0:T(8,128)} async-done(((f32[128,16384]{1,0:T(8,128)}), f32[512,16384]{1,0:T(8,128)}) %all-gather.3.cloned.1.call-update) | async-done | bytes 33554448 | tf_op jit(solution)/shard_map/all_gather | solution.py:9
  212.0 60.5 %fusion = f32[512,512]{1,0:T(8,128)} fusion(f32[512,16384]{1,0:T(8,128)} %all-gather.3.cloned.1.call-done, f32[512,16384]{1,0:T(8,128)} %param.4), kind=kOutput, calls=%fused_computation | convolution fusion | flops 51539607552 | bytes 68157440 | tf_op jit(solution)/shard_map/dot_general | solution.py:8
  272.4 0.0 reduce-scatter.3.cloned.1.call-update
  272.5 0.0 reduce-scatter.5.cloned.1.call-start
  272.5 62.4 %all-gather.5.cloned.1.call-done = f32[512,4096]{1,0:T(8,128)} async-done(((f32[64,4096]{1,0:T(8,128)}), f32[512,4096]{1,0:T(8,128)}) %all-gather.5.cloned.1.call-update) | async-done | bytes 8388624 | tf_op jit(solution)/shard_map/all_gather | solution.py:18
  334.9 67.0 %reduce-scatter.3.cloned.1.call-done = f32[64,512]{1,0:T(8,128)} async-done(((f32[512,512]{1,0:T(8,128)}), f32[64,512]{1,0:T(8,128)}) %reduce-scatter.3.cloned.1.call-update) | async-done | bytes 131088 | tf_op jit(solution)/shard_map/reduce_scatter | solution.py:15
  401.9 9.6 %fusion.1 = f32[64,4096]{1,0:T(8,128)} fusion(f32[64,512]{1,0:T(8,128)} %reduce-scatter.3.cloned.1.call-done, f32[512,4096]{1,0:T(8,128)} %all-gather.5.cloned.1.call-done), kind=kOutput, calls=%fused_computation.1 | convolution fusion | flops 1610612736 | bytes 9568256 | tf_op jit(solution)/shard_map/dot_general | solution.py:16
  411.4 0.0 reduce-scatter.5.cloned.1.call-update
  411.4 26.0 %reduce-scatter.5.cloned.1.call-done = f32[64,1024]{1,0:T(8,128)} async-done(((f32[64,4096]{1,0:T(8,128)}), f32[64,1024]{1,0:T(8,128)}) %reduce-scatter.5.cloned.1.call-update) | async-done | bytes 262160 | tf_op jit(solution)/shard_map/reduce_scatter | solution.py:22
Async XLA Ops:
  6.5 205.4 %all-gather.3.cloned.1.call-start = ((), (), s32[]{:S(2)}) async-start(), calls=%async_computation.2 | async-start | bytes 41943040 | tf_op jit(solution)/shard_map/all_gather | solution.py:9
  7.3 327.6 %all-gather.5.cloned.1.call-start = ((), (), s32[]{:S(2)}) async-start(), calls=%async_computation.4 | async-start | bytes 9437184 | tf_op jit(solution)/shard_map/all_gather | solution.py:18
  8.0 393.9 %reduce-scatter.3.cloned.1.call-start = ((), (), s32[]{:S(2)}) async-start(), calls=%async_computation.3 | async-start | bytes 1179648 | tf_op jit(solution)/shard_map/reduce_scatter | solution.py:15
  272.5 164.9 %reduce-scatter.5.cloned.1.call-start = ((), (), s32[]{:S(2)}) async-start(), calls=%async_computation.5 | async-start | bytes 1310720 | tf_op jit(solution)/shard_map/reduce_scatter | solution.py:22
Sparse Core Ops, SparseCore 0:
  8.9 203.0 all-gather.2
  214.1 120.7 all-gather.4
  338.3 63.5 reduce-scatter.2
  411.6 25.7 reduce-scatter.4
where the time goes:
time: 446 us; the launch traced here: 444 us
  waiting for transfers between devices  361 us (81%)
  matrix products  70.1 us (16%)
  between operations  13.1 us (3%)
    all_gather x1, waiting for transfers between devices, per_device(): lax.all_gather(green_vectors, 'row', axis=0, tiled=True)  204 us
    reduce_scatter x1, waiting for transfers between devices, per_device(): lax.psum_scatter(partial_terms, 'col', scatter_dimension=0, tiled=True)  67 us
    all_gather x1, waiting for transfers between devices, per_device(): lax.all_gather(cholesky, 'col', axis=0, tiled=True)  62.4 us
    dot_general x1, matrix products, per_device(): lax.dot_general(lax.all_gather(green_vectors, 'row', axis=0, tiled=True),...  60.5 us
    reduce_scatter x1, waiting for transfers between devices, per_device(): return lax.psum_scatter(row_terms, 'row', scatter_dimension=1, tiled=True)  26 us
    dot_general x1, matrix products, per_device(): jnp.dot(local_walkers, lax.all_gather(cholesky, 'col', axis=0, tiled=True...  9.56 us
  transfers between devices with their start and end apart: 4, of which 4 were waited for; matrix products, arithmetic and copies ran while one was open for 14% of the time, Pallas kernels for 0%

commit v1 on v0

v1 whole, which is shorter than its diff:
```python
import jax
import jax.numpy as jnp
from jax import lax
from jax.sharding import PartitionSpec as P

CHUNKS = 4


def three_pass(left, right, dims):
    return lax.dot_general(
        left,
        right,
        (dims, ((), ())),
        precision=lax.Precision.HIGH,
        preferred_element_type=jnp.float32,
    )


def per_device(green_vectors, amplitudes, cholesky):
    rows = lax.axis_size("row")
    me = lax.axis_index("row")
    held, pairs = green_vectors.shape
    width = pairs // CHUNKS
    sibling = [(i, i ^ 1) for i in range(rows)]

    def part(array, c):
        return lax.slice_in_dim(array, c * width, (c + 1) * width, axis=1)

    far = [
        [
            lax.ppermute(part(green_vectors, c), "row", [(i, (i + hop) % rows) for i in range(rows)])
            for hop in range(2, rows, 2)
        ]
        for c in range(CHUNKS)
    ]
    near = lax.ppermute(green_vectors, "row", sibling)
    stacked = lax.all_gather(cholesky, "col", axis=0, tiled=True)
    last = ((1,), (1,))

    def terms(block, other, slab):
        return three_pass(jnp.concatenate([block, other], axis=0), slab, last)

    sums = [terms(green_vectors, near, amplitudes)]
    for c in range(CHUNKS):
        for at, piece in enumerate(far[c]):
            crossed = lax.ppermute(piece, "row", sibling)
            if c == CHUNKS - 1 and at == 0:
                crossed, stacked = lax.optimization_barrier((crossed, stacked))
            term = terms(piece, crossed, part(amplitudes, c))
            if c == 0:
                sums.append(term)
            else:
                sums[at + 1] += term
    total = jnp.zeros((rows * held, amplitudes.shape[0]), jnp.float32)
    for at, block in enumerate(sums):
        for side in range(2):
            owner = lax.rem(me - 2 * at + rows, rows) ^ side
            total = lax.dynamic_update_slice(
                total, lax.slice_in_dim(block, side * held, (side + 1) * held, axis=0), (owner * held, 0)
            )
    local_walkers = lax.psum_scatter(total, "col", scatter_dimension=0, tiled=True)
    row_terms = three_pass(local_walkers, stacked, ((1,), (0,)))
    return lax.psum_scatter(row_terms, "row", scatter_dimension=1, tiled=True)


def solution(mesh):
    placed = (P("row", "col"), P("row", "col"), P(("row", "col"), None))
    return jax.shard_map(
        per_device, mesh=mesh, in_specs=placed, out_specs=P("col", "row"), check_vma=False
    )
```

time: 446 us -> 355 us (0.80)
  waiting for transfers between devices: 361 us -> 265 us
  matrix products: 70.1 us -> 58.6 us
  starting transfers between devices: 0.12 us -> 8.59 us
  local copies, waits for them, and re-layouts: 0 us -> 7.54 us
    all_gather x2 -> x1, waiting for transfers between devices: 266 us -> 0.02 us  [per_device(): stacked = lax.all_gather(cholesky, 'col', axis=0, tiled=True)]
    ppermute x0 -> x9, waiting for transfers between devices: none -> 175 us  [the longest x4 175 us: per_device(): lax.ppermute(part(green_vectors, c), 'row', [(i, (i + hop) % rows) for i...]
    dot_general x2 -> x6, matrix products: 70.1 us -> 58.6 us  [three_pass(): lax.dot_general(left, right, (dims, ((), ())), precision=lax.Precision.HI...]
    ppermute x0 -> x9, starting transfers between devices: none -> 8.51 us  [the longest x4 4.84 us: per_device(): crossed = lax.ppermute(piece, 'row', sibling)]
    slice x0 -> x1, local copies, waits for them, and re-layouts: none -> 6.27 us  [part(): return lax.slice_in_dim(array, c * width, (c + 1) * width, axis=1)]
  transfers between devices with their start and end apart: 4 -> 12, of which waited for: 4 -> 6; matrix products, arithmetic and copies ran while one was open for 14% -> 14% of each run, Pallas kernels for 0% -> 0%
where the time goes in v1:
time: 355 us; the launch traced here: 353 us
  waiting for transfers between devices  265 us (75%)
  matrix products  58.6 us (17%)
  between operations  13.2 us (4%)
  starting transfers between devices  8.59 us (2%)
  local copies, waits for them, and re-layouts  7.54 us (2%)
    ppermute x4, waiting for transfers between devices, per_device(): lax.ppermute(part(green_vectors, c), 'row', [(i, (i + hop) % rows) for i...  175 us
    reduce_scatter x1, waiting for transfers between devices, per_device(): lax.psum_scatter(total, 'col', scatter_dimension=0, tiled=True)  62.8 us
    dot_general x6, matrix products, three_pass(): lax.dot_general(left, right, (dims, ((), ())), precision=lax.Precision.HI...  58.6 us
    reduce_scatter x1, waiting for transfers between devices, per_device(): return lax.psum_scatter(row_terms, 'row', scatter_dimension=1, tiled=True)  26 us
  transfers between devices with their start and end apart: 12, of which 6 were waited for; matrix products, arithmetic and copies ran while one was open for 14% of the time, Pallas kernels for 0%

profile of v1, /device:TPU:13, one launch (start us, length us, event | category | flops | bytes accessed | tf_op | source)
XLA Modules:
  0.0 352.7 jit_solution(7127198597602883471)
XLA Ops:
  6.5 0.0 all-gather.2.cloned.1.call-start
  6.5 0.7 all-gather.2.cloned.1.call-update
  7.3 0.0 reduce-scatter.3.cloned.1.call-start
  7.3 0.7 collective-permute-start
  8.0 6.3 %fusion.44 = (f32[128,4096]{1,0:T(8,128)}, f32[128,4096]{1,0:T(8,128)S(1)}, f32[128,4096]{1,0:T(8,128)}, f32[128,4096]{1,0:T(8,128)S(1)}) fusion(f32[128,16384]{1,0:T(8,128)} %param.3), kind=kLoop, calls=%fused_computation.36 | loop fusion | bytes 16777216 | tf_op jit(solution)/shard_map/slice | solution.py:27
  14.3 1.2 collective-permute-start.5
  15.5 0.3 collective-permute-start.3
  15.8 1.2 collective-permute-start.7
  17.0 0.3 collective-permute-start.1
  17.2 44.3 %collective-permute-done.5 = f32[128,4096]{1,0:T(8,128)} collective-permute-done((f32[128,4096]{1,0:T(8,128)S(1)}, f32[128,4096]{1,0:T(8,128)}, u32[]{:S(2)}, u32[]{:S(2)}) %collective-permute-start.5) | collective-permute-done | bytes 2097184 | tf_op jit(solution)/shard_map/ppermute | solution.py:31
  61.6 1.4 collective-permute-start.6
  62.9 43.6 %collective-permute-done.3 = f32[128,4096]{1,0:T(8,128)S(1)} collective-permute-done((f32[128,4096]{1,0:T(8,128)S(1)}, f32[128,4096]{1,0:T(8,128)S(1)}, u32[]{:S(2)}, u32[]{:S(2)}) %collective-permute-start.3) | collective-permute-done | bytes 2097184 | tf_op jit(solution)/shard_map/ppermute | solution.py:31
  106.5 1.2 collective-permute-start.4
  107.8 43.7 %collective-permute-done.7 = f32[128,4096]{1,0:T(8,128)} collective-permute-done((f32[128,4096]{1,0:T(8,128)}, f32[128,4096]{1,0:T(8,128)}, u32[]{:S(2)}, u32[]{:S(2)}) %collective-permute-start.7) | collective-permute-done | bytes 2097184 | tf_op jit(solution)/shard_map/ppermute | solution.py:31
  151.5 1.4 collective-permute-start.8
  152.8 43.6 %collective-permute-done.1 = f32[128,4096]{1,0:T(8,128)} collective-permute-done((f32[128,4096]{1,0:T(8,128)}, f32[128,4096]{1,0:T(8,128)}, u32[]{:S(2)}, u32[]{:S(2)}) %collective-permute-start.1) | collective-permute-done | bytes 2097184 | tf_op jit(solution)/shard_map/ppermute | solution.py:31
  196.4 0.9 collective-permute-start.2
  197.3 0.0 collective-permute-done.6
  197.3 7.6 %fusion.6 = f32[256,512]{1,0:T(8,128)S(1)} fusion(f32[512,16384]{1,0:T(8,128)} %param.4, f32[128,4096]{1,0:T(8,128)} %collective-permute-done.6, f32[128,4096]{1,0:T(8,128)} %collective-permute-done.5), kind=kOutput, calls=%fused_computation.6 | convolution fusion | flops 3222274048 | bytes 13107200 | tf_op jit(solution)/shard_map/dot_general | solution.py:10
  204.9 0.0 collective-permute-done.4
  204.9 7.0 %fusion.8 = f32[256,512]{1,0:T(8,128)S(1)} fusion(f32[512,16384]{1,0:T(8,128)} %param.4, f32[128,4096]{1,0:T(8,128)} %collective-permute-done.4, f32[128,4096]{1,0:T(8,128)S(1)} %collective-permute-done.3), kind=kOutput, calls=%fused_computation.8 | convolution fusion | flops 3222274048 | bytes 13107200 | tf_op jit(solution)/shard_map/dot_general | solution.py:10
  212.0 0.0 collective-permute-done
  212.0 21.0 %fusion = f32[256,512]{1,0:T(8,128)S(1)} fusion(f32[512,16384]{1,0:T(8,128)} %param.4, f32[128,16384]{1,0:T(8,128)} %collective-permute-done, f32[128,16384]{1,0:T(8,128)} %param.3), kind=kOutput, calls=%fused_computation | convolution fusion | flops 12889096192 | bytes 50855936 | tf_op jit(solution)/shard_map/dot_general | solution.py:10
  233.0 0.1 broadcast_in_dim.3
  233.2 0.0 collective-permute-done.8
  233.2 0.0 all-gather.2.cloned.1.call-done
  233.2 7.7 %fusion.4 = f32[256,512]{1,0:T(8,128)S(1)} fusion(f32[512,16384]{1,0:T(8,128)} %param.4, f32[128,4096]{1,0:T(8,128)} %collective-permute-done.8, f32[128,4096]{1,0:T(8,128)} %collective-permute-done.7), kind=kOutput, calls=%fused_computation.4 | convolution fusion | flops 3222274048 | bytes 13107200 | tf_op jit(solution)/shard_map/dot_general | solution.py:10
  240.9 0.0 collective-permute-done.2
  240.9 7.9 %fusion.34 = f32[256,512]{1,0:T(8,128)S(1)} fusion(f32[256,512]{1,0:T(8,128)S(1)} %fusion.4, f32[256,512]{1,0:T(8,128)S(1)} %fusion.6, f32[256,512]{1,0:T(8,128)S(1)} %fusion.8, f32[512,16384]{1,0:T(8,128)} %param.4, f32[128,4096]{1,0:T(8,128)} %collective-permute-done.2, f32[128,4096]{1,0:T(8,128)} %collective-permute-done.1), kind=kOutput, calls=%fused_computation.26 | convolution fusion | flops 3222667264 | bytes 14680064 | tf_op jit(solution)/shard_map/dot_general | solution.py:10
  248.9 0.0 copy-start
  248.9 1.1 copy-done
  249.9 0.0 reduce-scatter.3.cloned.1.call-update
  249.9 0.0 reduce-scatter.5.cloned.1.call-start
  250.0 62.8 %reduce-scatter.3.cloned.1.call-done = f32[64,512]{1,0:T(8,128)} async-done(((f32[512,512]{1,0:T(8,128)}), f32[64,512]{1,0:T(8,128)}) %reduce-scatter.3.cloned.1.call-update) | async-done | bytes 131088 | tf_op jit(solution)/shard_map/reduce_scatter | solution.py:61
  312.8 7.4 %fusion.45 = f32[64,4096]{1,0:T(8,128)} fusion(f32[64,512]{1,0:T(8,128)} %reduce-scatter.3.cloned.1.call-done, f32[512,4096]{1,0:T(8,128)} %all-gather.2.cloned.1.call-done), kind=kOutput, calls=%fused_computation.37 | convolution fusion | flops 805306368 | bytes 9568256 | tf_op jit(solution)/shard_map/dot_general | solution.py:10
  320.1 0.0 reduce-scatter.5.cloned.1.call-update
  320.2 26.0 %reduce-scatter.5.cloned.1.call-done = f32[64,1024]{1,0:T(8,128)} async-done(((f32[64,4096]{1,0:T(8,128)}), f32[64,1024]{1,0:T(8,128)}) %reduce-scatter.5.cloned.1.call-update) | async-done | bytes 262160 | tf_op jit(solution)/shard_map/reduce_scatter | solution.py:63
  (4 shorter events, 0.1 us)
Async XLA Ops:
  6.5 226.7 %all-gather.2.cloned.1.call-start = ((), (), s32[]{:S(2)}) async-start(), calls=%async_computation.2 | async-start | bytes 9437184 | tf_op jit(solution)/shard_map/all_gather | solution.py:37
  7.3 305.5 %reduce-scatter.3.cloned.1.call-start = ((), (), s32[]{:S(2)}) async-start(), calls=%async_computation.3 | async-start | bytes 1179648 | tf_op jit(solution)/shard_map/reduce_scatter | solution.py:61
  7.3 204.7 %collective-permute-start = (f32[128,16384]{1,0:T(8,128)}, f32[128,16384]{1,0:T(8,128)}, u32[]{:S(2)}, u32[]{:S(2)}) collective-permute-start(f32[128,16384]{1,0:T(8,128)} %param.3), channel_id=1, source_target_pairs={{0,8},{8,0},{16,24},{24,16},{1,9},{9,1},{17,25},{25,17},{2,10},{10... | collective-permute-start | bytes 25165832 | tf_op jit(solution)/shard_map/ppermute | solution.py:36
  14.3 47.3 %collective-permute-start.5 = (f32[128,4096]{1,0:T(8,128)S(1)}, f32[128,4096]{1,0:T(8,128)}, u32[]{:S(2)}, u32[]{:S(2)}) collective-permute-start(f32[128,4096]{1,0:T(8,128)S(1)} %get-tuple-element.12), channel_id=1, source_target_pairs={{0,16},{8,24},{16,0},{24,8},{1,17},{9,25},{17,1},{25,9},{2,18},{10... | collective-permute-start | bytes 6291464 | tf_op jit(solution)/shard_map/ppermute | solution.py:31
  15.5 91.0 %collective-permute-start.3 = (f32[128,4096]{1,0:T(8,128)S(1)}, f32[128,4096]{1,0:T(8,128)S(1)}, u32[]{:S(2)}, u32[]{:S(2)}) collective-permute-start(f32[128,4096]{1,0:T(8,128)S(1)} %get-tuple-element.10), channel_id=1, source_target_pairs={{0,16},{8,24},{16,0},{24,8},{1,17},{9,25},{17,1},{25,9},{2,18},{10... | collective-permute-start | bytes 6291464 | tf_op jit(solution)/shard_map/ppermute | solution.py:31
  15.8 135.7 %collective-permute-start.7 = (f32[128,4096]{1,0:T(8,128)}, f32[128,4096]{1,0:T(8,128)}, u32[]{:S(2)}, u32[]{:S(2)}) collective-permute-start(f32[128,4096]{1,0:T(8,128)} %get-tuple-element.11), channel_id=1, source_target_pairs={{0,16},{8,24},{16,0},{24,8},{1,17},{9,25},{17,1},{25,9},{2,18},{10... | collective-permute-start | bytes 6291464 | tf_op jit(solution)/shard_map/ppermute | solution.py:31
  17.0 179.4 %collective-permute-start.1 = (f32[128,4096]{1,0:T(8,128)}, f32[128,4096]{1,0:T(8,128)}, u32[]{:S(2)}, u32[]{:S(2)}) collective-permute-start(f32[128,4096]{1,0:T(8,128)} %get-tuple-element.9), channel_id=1, source_target_pairs={{0,16},{8,24},{16,0},{24,8},{1,17},{9,25},{17,1},{25,9},{2,18},{10... | collective-permute-start | bytes 6291464 | tf_op jit(solution)/shard_map/ppermute | solution.py:31
  61.6 135.7 %collective-permute-start.6 = (f32[128,4096]{1,0:T(8,128)}, f32[128,4096]{1,0:T(8,128)}, u32[]{:S(2)}, u32[]{:S(2)}) collective-permute-start(f32[128,4096]{1,0:T(8,128)} %collective-permute-done.5), channel_id=1, source_target_pairs={{0,8},{8,0},{16,24},{24,16},{1,9},{9,1},{17,25},{25,17},{2,10},{10... | collective-permute-start | bytes 6291464 | tf_op jit(solution)/shard_map/ppermute | solution.py:46
  106.5 98.4 %collective-permute-start.4 = (f32[128,4096]{1,0:T(8,128)S(1)}, f32[128,4096]{1,0:T(8,128)}, u32[]{:S(2)}, u32[]{:S(2)}) collective-permute-start(f32[128,4096]{1,0:T(8,128)S(1)} %collective-permute-done.3), channel_id=1, source_target_pairs={{0,8},{8,0},{16,24},{24,16},{1,9},{9,1},{17,25},{25,17},{2,10},{10... | collective-permute-start | bytes 6291464 | tf_op jit(solution)/shard_map/ppermute | solution.py:46
  151.5 81.7 %collective-permute-start.8 = (f32[128,4096]{1,0:T(8,128)}, f32[128,4096]{1,0:T(8,128)}, u32[]{:S(2)}, u32[]{:S(2)}) collective-permute-start(f32[128,4096]{1,0:T(8,128)} %collective-permute-done.7), channel_id=1, source_target_pairs={{0,8},{8,0},{16,24},{24,16},{1,9},{9,1},{17,25},{25,17},{2,10},{10... | collective-permute-start | bytes 6291464 | tf_op jit(solution)/shard_map/ppermute | solution.py:46
  196.4 44.5 %collective-permute-start.2 = (f32[128,4096]{1,0:T(8,128)}, f32[128,4096]{1,0:T(8,128)}, u32[]{:S(2)}, u32[]{:S(2)}) collective-permute-start(f32[128,4096]{1,0:T(8,128)} %collective-permute-done.1), channel_id=1, source_target_pairs={{0,8},{8,0},{16,24},{24,16},{1,9},{9,1},{17,25},{25,17},{2,10},{10... | collective-permute-start | bytes 6291464 | tf_op jit(solution)/shard_map/ppermute | solution.py:46
  248.9 1.1 copy-start
  249.9 96.2 %reduce-scatter.5.cloned.1.call-start = ((), (), s32[]{:S(2)}) async-start(), calls=%async_computation.4 | async-start | bytes 1310720 | tf_op jit(solution)/shard_map/reduce_scatter | solution.py:63
Sparse Core Ops, SparseCore 0:
  9.5 122.2 all-gather.1
  250.1 62.6 reduce-scatter.2
  320.3 25.8 reduce-scatter.4

commit v2 on v1

v2 whole, which is shorter than its diff:
```python
import functools

import jax
import jax.numpy as jnp
from jax import lax
from jax.experimental import pallas as pl
from jax.experimental.pallas import tpu as pltpu
from jax.sharding import PartitionSpec as P

SHARES = (6, 5, 3, 2)
MESH = pl.DeviceIdType.MESH


def three_pass(left, right, dims):
    return lax.dot_general(
        left,
        right,
        (dims, ((), ())),
        precision=lax.Precision.HIGH,
        preferred_element_type=jnp.float32,
    )


def halves(x):
    high = x.astype(jnp.bfloat16)
    return high, (x - high.astype(jnp.float32)).astype(jnp.bfloat16)


def tail_kernel(
    rows, cols, total, chol, out, landed, slab, leaving, arrived,
    send_sem, recv_sem, load_sem, row_send, row_recv,
):
    row, col = lax.axis_index("row"), lax.axis_index("col")
    quarter = out.shape[1]
    walkers = out.shape[0]

    barrier = pltpu.get_barrier_semaphore()
    for k in range(1, cols):
        pl.semaphore_signal(barrier, inc=1, device_id=(row, lax.rem(col + k, cols)), device_id_type=MESH)
    for m in range(1, rows):
        pl.semaphore_signal(barrier, inc=1, device_id=(lax.rem(row + m, rows), col), device_id_type=MESH)
    order = [rows // 2] + [m for m in range(1, rows) if m != rows // 2] + [0]
    loads = {}
    for m in order:
        start = pl.multiple_of(lax.rem(row + m, rows) * quarter, quarter)
        loads[m] = pltpu.make_async_copy(chol.at[:, pl.ds(start, quarter)], slab.at[m], load_sem.at[m])
    own = pltpu.make_async_copy(total.at[col], landed.at[0], recv_sem.at[0])
    own.start()
    for m in order:
        loads[m].start()
    pl.semaphore_wait(barrier, rows + cols - 2)

    copies = []
    for k in range(1, cols):
        target = lax.rem(col + k, cols)
        copy = pltpu.make_async_remote_copy(
            src_ref=total.at[target],
            dst_ref=landed.at[k],
            send_sem=send_sem.at[k],
            recv_sem=recv_sem.at[k],
            device_id=(row, target),
            device_id_type=MESH,
        )
        copy.start()
        copies.append(copy)
    own.wait()
    effective = landed[0]
    for k, copy in enumerate(copies):
        copy.wait_recv()
        effective = effective + landed[k + 1]
    high, low = halves(effective)
    both = jnp.concatenate([high, low], axis=0)

    tile = min(512, quarter)
    sends = []
    for m in order:
        loads[m].wait()
        for t in range(0, quarter, tile):
            right_high, right_low = halves(slab[m, :, t : t + tile])
            pair = jnp.dot(both, right_high, preferred_element_type=jnp.float32)
            rest = jnp.dot(high, right_low, preferred_element_type=jnp.float32)
            leaving[m, :, t : t + tile] = pair[:walkers] + (pair[walkers:] + rest)
        if m:
            send = pltpu.make_async_remote_copy(
                src_ref=leaving.at[m],
                dst_ref=arrived.at[m],
                send_sem=row_send.at[m],
                recv_sem=row_recv.at[m],
                device_id=(lax.rem(row + m, rows), col),
                device_id_type=MESH,
            )
            send.start()
            sends.append((m, send))
    result = leaving[0]
    for m, send in sends:
        send.wait_recv()
        result = result + arrived[m]
    out[...] = result
    for copy in copies:
        copy.wait_send()
    for m, send in sends:
        send.wait_send()


def tail(total, chol):
    rows, cols = lax.axis_size("row"), lax.axis_size("col")
    walkers, depth = total.shape[0] // cols, total.shape[1]
    quarter = chol.shape[1] // rows
    f32 = jnp.float32
    return pl.pallas_call(
        functools.partial(tail_kernel, rows, cols),
        out_shape=jax.ShapeDtypeStruct((walkers, quarter), f32),
        in_specs=[pl.BlockSpec(memory_space=pl.ANY)] * 2,
        out_specs=pl.BlockSpec(memory_space=pltpu.VMEM),
        scratch_shapes=[
            pltpu.VMEM((cols, walkers, depth), f32),
            pltpu.VMEM((rows, depth, quarter), f32),
            pltpu.VMEM((rows, walkers, quarter), f32),
            pltpu.VMEM((rows, walkers, quarter), f32),
            pltpu.SemaphoreType.DMA((cols,)),
            pltpu.SemaphoreType.DMA((cols,)),
            pltpu.SemaphoreType.DMA((rows,)),
            pltpu.SemaphoreType.DMA((rows,)),
            pltpu.SemaphoreType.DMA((rows,)),
        ],
        compiler_params=pltpu.CompilerParams(
            collective_id=0, has_side_effects=True, vmem_limit_bytes=32 * 1024 * 1024
        ),
    )(total.reshape(cols, walkers, depth), chol)


def per_device(green_vectors, amplitudes, cholesky):
    rows = lax.axis_size("row")
    me = lax.axis_index("row")
    held, pairs = green_vectors.shape
    sibling = [(i, i ^ 1) for i in range(rows)]
    hops = range(2, rows, 2)
    cuts = [0]
    for share in SHARES:
        cuts.append(cuts[-1] + share * pairs // sum(SHARES))

    def part(array, c):
        return lax.slice_in_dim(array, cuts[c], cuts[c + 1], axis=1)

    def far(piece):
        return [lax.ppermute(piece, "row", [(i, (i + hop) % rows) for i in range(rows)]) for hop in hops]

    def terms(block, other, slab):
        return three_pass(jnp.concatenate([block, other], axis=0), slab, ((1,), (1,)))

    def cross(pieces):
        return [lax.ppermute(piece, "row", sibling) for piece in pieces]

    def dots(pieces, crossed, c):
        return [terms(a, b, part(amplitudes, c)) for a, b in zip(pieces, crossed)]

    first, second = far(part(green_vectors, 0)), far(part(green_vectors, 1))
    stacked = lax.all_gather(cholesky, "col", axis=0, tiled=True)
    near = lax.ppermute(green_vectors, "row", sibling)
    own = terms(green_vectors, near, amplitudes)
    piece, own = lax.optimization_barrier((part(green_vectors, 2), own))
    third = far(piece)
    second, own = lax.optimization_barrier((second, own))
    sums = dots(first, cross(first), 0)
    piece, sums = lax.optimization_barrier((part(green_vectors, 3), sums))
    fourth = far(piece)
    third, sums = lax.optimization_barrier((third, sums))
    for c, pieces in ((1, second), (2, third)):
        sums = [a + b for a, b in zip(sums, dots(pieces, cross(pieces), c))]
        if c == 2:
            fourth, sums, stacked = lax.optimization_barrier((fourth, sums, stacked))
    sums = [a + b for a, b in zip(sums, dots(fourth, cross(fourth), 3))]

    total = jnp.zeros((rows * held, amplitudes.shape[0]), jnp.float32)
    for at, block in enumerate([own] + sums):
        for side in range(2):
            owner = lax.rem(me - 2 * at + rows, rows) ^ side
            total = lax.dynamic_update_slice(
                total, lax.slice_in_dim(block, side * held, (side + 1) * held, axis=0), (owner * held, 0)
            )
    return tail(total, stacked)


def solution(mesh):
    placed = (P("row", "col"), P("row", "col"), P(("row", "col"), None))
    return jax.shard_map(
        per_device, mesh=mesh, in_specs=placed, out_specs=P("col", "row"), check_vma=False
    )
```

time: 355 us -> 255 us (0.72)
  waiting for transfers between devices: 265 us -> 129 us
  Pallas kernels: 0 us -> 41.3 us
  matrix products: 58.6 us -> 49.7 us
    reduce_scatter x2 -> x0, waiting for transfers between devices: 88.7 us -> none  [the longest x1 62.8 us: per_device(): lax.psum_scatter(total, 'col', scatter_dimension=0, tiled=True)]
    ppermute x8, waiting for transfers between devices: 175 us -> 129 us  [the longest x4 127 us: far(): lax.ppermute(piece, 'row', [(i, (i + hop) % rows) for i in range(rows)])]
    pallas_call x0 -> x1, Pallas kernels: none -> 41.3 us  [tail(): pl.pallas_call(functools.partial(tail_kernel, rows, cols), out_shape=jax....]
    dot_general x6 -> x5, matrix products: 58.6 us -> 49.7 us  [three_pass(): lax.dot_general(left, right, (dims, ((), ())), precision=lax.Precision.HI...]
    slice x1 -> x4, local copies, waits for them, and re-layouts: 6.27 us -> 9.67 us  [part(): return lax.slice_in_dim(array, cuts[c], cuts[c + 1], axis=1)]
  transfers between devices with their start and end apart: 12 -> 10, of which waited for: 6 -> 5; matrix products, arithmetic and copies ran while one was open for 14% -> 22% of each run, Pallas kernels for 0% -> 0%
where the time goes in v2:
time: 255 us; the launch traced here: 254 us
  waiting for transfers between devices  129 us (51%)
  matrix products  49.7 us (19%)
  Pallas kernels  41.3 us (16%)
  between operations  13.5 us (5%)
  local copies, waits for them, and re-layouts  10.6 us (4%)
  starting transfers between devices  10.4 us (4%)
    ppermute x4, waiting for transfers between devices, far(): lax.ppermute(piece, 'row', [(i, (i + hop) % rows) for i in range(rows)])  127 us
    dot_general x5, matrix products, three_pass(): lax.dot_general(left, right, (dims, ((), ())), precision=lax.Precision.HI...  49.7 us
    pallas_call x1, Pallas kernels, tail(): pl.pallas_call(functools.partial(tail_kernel, rows, cols), out_shape=jax....  41.3 us
    slice x4, local copies, waits for them, and re-layouts, part(): return lax.slice_in_dim(array, cuts[c], cuts[c + 1], axis=1)  9.67 us
    ppermute x4, starting transfers between devices, cross(): return [lax.ppermute(piece, 'row', sibling) for piece in pieces]  5.81 us
  transfers between devices with their start and end apart: 10, of which 5 were waited for; matrix products, arithmetic and copies ran while one was open for 22% of the time, Pallas kernels for 0%

profile of v2, /device:TPU:13, one launch (start us, length us, event | category | flops | bytes accessed | tf_op | source)
XLA Modules:
  0.0 254.4 jit_solution(12749945163468311093)
XLA Ops:
  6.5 0.0 all-gather.2.cloned.1.call-start
  6.5 0.7 collective-permute-start.1
  7.2 0.0 all-gather.2.cloned.1.call-update
  7.3 2.1 slice.41
  9.4 1.3 collective-permute-start.2
  10.7 3.5 %slice.36 = f32[128,5120]{1,0:T(8,128)} slice(f32[128,16384]{1,0:T(8,128)} %param.3), slice={[0:128], [6144:11264]} | slice | bytes 5242880 | tf_op jit(solution)/shard_map/slice | solution.py:143
  14.2 0.3 collective-permute-start
  14.4 2.8 %slice.37 = f32[128,3072]{1,0:T(8,128)} slice(f32[128,16384]{1,0:T(8,128)} %param.3), slice={[0:128], [11264:14336]} | slice | bytes 3145728 | tf_op jit(solution)/shard_map/slice | solution.py:143
  17.2 61.4 %collective-permute-done.2 = f32[128,6144]{1,0:T(8,128)S(1)} collective-permute-done((f32[128,6144]{1,0:T(8,128)S(1)}, f32[128,6144]{1,0:T(8,128)S(1)}, u32[]{:S(2)}, u32[]{:S(2)}) %collective-permute-start.2) | collective-permute-done | bytes 3145760 | tf_op jit(solution)/shard_map/ppermute | solution.py:146
  78.5 2.6 %collective-permute-start.3 = (f32[128,6144]{1,0:T(8,128)S(1)}, f32[128,6144]{1,0:T(8,128)}, u32[]{:S(2)}, u32[]{:S(2)}) collective-permute-start(f32[128,6144]{1,0:T(8,128)S(1)} %collective-permute-done.2), channel_id=1, source_target_pairs={{0,8},{8,0},{16,24},{24,16},{1,9},{9,1},{17,25},{25,17},{2,10},{10... | collective-permute-start | bytes 9437192 | tf_op jit(solution)/shard_map/ppermute | solution.py:152
  81.1 0.0 collective-permute-done.1
  81.1 21.8 %fusion = f32[256,512]{1,0:T(8,128)} fusion(f32[512,16384]{1,0:T(8,128)} %param.4, f32[128,16384]{1,0:T(8,128)} %collective-permute-done.1, f32[128,16384]{1,0:T(8,128)} %param.3), kind=kOutput, calls=%fused_computation | convolution fusion | flops 12889096192 | bytes 50855936 | tf_op jit(solution)/shard_map/dot_general | solution.py:15
  102.9 31.8 %collective-permute-done = f32[128,5120]{1,0:T(8,128)} collective-permute-done((f32[128,5120]{1,0:T(8,128)}, f32[128,5120]{1,0:T(8,128)}, u32[]{:S(2)}, u32[]{:S(2)}) %collective-permute-start) | collective-permute-done | bytes 2621472 | tf_op jit(solution)/shard_map/ppermute | solution.py:146
  134.7 1.5 collective-permute-start.6
  136.3 1.2 collective-permute-start.5
  137.5 1.3 slice.40
  138.8 0.0 collective-permute-done.3
  138.8 9.6 %fusion.4 = f32[256,512]{1,0:T(8,128)S(1)} fusion(f32[512,16384]{1,0:T(8,128)} %param.4, f32[128,6144]{1,0:T(8,128)} %collective-permute-done.3, f32[128,6144]{1,0:T(8,128)S(1)} %collective-permute-done.2), kind=kOutput, calls=%fused_computation.4 | convolution fusion | flops 4833411072 | bytes 19398656 | tf_op jit(solution)/shard_map/dot_general | solution.py:15
  148.4 24.0 %collective-permute-done.5 = f32[128,3072]{1,0:T(8,128)S(1)} collective-permute-done((f32[128,3072]{1,0:T(8,128)}, f32[128,3072]{1,0:T(8,128)S(1)}, u32[]{:S(2)}, u32[]{:S(2)}) %collective-permute-start.5) | collective-permute-done | bytes 1572896 | tf_op jit(solution)/shard_map/ppermute | solution.py:146
  172.4 0.9 collective-permute-start.7
  173.3 1.2 collective-permute-start.4
  174.5 0.0 collective-permute-done.6
  174.5 8.5 %fusion.6 = f32[256,512]{1,0:T(8,128)S(1)} fusion(f32[512,16384]{1,0:T(8,128)} %param.4, f32[128,5120]{1,0:T(8,128)S(1)} %collective-permute-done.6, f32[128,5120]{1,0:T(8,128)} %collective-permute-done), kind=kOutput, calls=%fused_computation.6 | convolution fusion | flops 4027842560 | bytes 16252928 | tf_op jit(solution)/shard_map/dot_general | solution.py:15
  183.0 0.0 copy-start.1
  183.0 0.0 collective-permute-done.7
  183.0 5.5 %add_add_fusion = f32[256,512]{1,0:T(8,128)S(1)} fusion(f32[256,512]{1,0:T(8,128)S(1)} %fusion.4, f32[256,512]{1,0:T(8,128)S(1)} %fusion.6, f32[512,16384]{1,0:T(8,128)} %param.4, f32[128,3072]{1,0:T(8,128)S(1)} %collective-permute-done.7, f32[128,3072]{1,0:T(8,128)S(1)} %collective-permute-done.5), kind=kOutput, calls=%fused_computation.24 | convolution fusion | flops 2416967680 | bytes 11010048 | tf_op jit(solution)/shard_map/dot_general | solution.py:15
  188.6 9.4 %collective-permute-done.4 = f32[128,2048]{1,0:T(8,128)S(1)} collective-permute-done((f32[128,2048]{1,0:T(8,128)S(1)}, f32[128,2048]{1,0:T(8,128)S(1)}, u32[]{:S(2)}, u32[]{:S(2)}) %collective-permute-start.4) | collective-permute-done | bytes 1048608 | tf_op jit(solution)/shard_map/ppermute | solution.py:146
  198.0 0.0 all-gather.2.cloned.1.call-done.chol
  198.0 0.9 collective-permute-start.8
  198.9 0.1 broadcast_in_dim.3
  199.0 0.0 copy-done.1
  199.0 0.0 copy-start
  199.1 2.1 collective-permute-done.8
  201.1 4.2 %fusion.16 = f32[256,512]{1,0:T(8,128)S(1)} fusion(f32[512,16384]{1,0:T(8,128)} %param.4, f32[128,2048]{1,0:T(8,128)S(1)} %collective-permute-done.8, f32[128,2048]{1,0:T(8,128)S(1)} %collective-permute-done.4), kind=kOutput, calls=%fused_computation.16 | convolution fusion | flops 1611137024 | bytes 6815744 | tf_op jit(solution)/shard_map/dot_general | solution.py:15
  205.4 0.1 add.37
  205.5 0.0 copy-done
  205.6 41.3 %shard_map.37 = f32[64,1024]{1,0:T(8,128)S(1)} custom-call(f32[8,64,512]{2,1,0:T(8,128)S(1)} %bitcast.2, f32[512,4096]{1,0:T(8,128)S(1)} %copy-done), custom_call_target="tpu_custom_call" | custom-call | tf_op jit(solution)/shard_map/pallas_call | solution.py:110
  246.9 0.7 copy.9
  (4 shorter events, 0.1 us)
Async XLA Ops:
  6.5 191.5 %all-gather.2.cloned.1.call-start = ((), (), s32[]{:S(2)}) async-start(), calls=%async_computation | async-start | bytes 9437184 | tf_op jit(solution)/shard_map/all_gather | solution.py:158
  6.5 74.6 %collective-permute-start.1 = (f32[128,16384]{1,0:T(8,128)}, f32[128,16384]{1,0:T(8,128)}, u32[]{:S(2)}, u32[]{:S(2)}) collective-permute-start(f32[128,16384]{1,0:T(8,128)} %param.3), channel_id=1, source_target_pairs={{0,8},{8,0},{16,24},{24,16},{1,9},{9,1},{17,25},{25,17},{2,10},{10... | collective-permute-start | bytes 25165832 | tf_op jit(solution)/shard_map/ppermute | solution.py:159
  9.4 69.2 %collective-permute-start.2 = (f32[128,6144]{1,0:T(8,128)S(1)}, f32[128,6144]{1,0:T(8,128)S(1)}, u32[]{:S(2)}, u32[]{:S(2)}) collective-permute-start(f32[128,6144]{1,0:T(8,128)S(1)} %slice.41), channel_id=1, source_target_pairs={{0,16},{8,24},{16,0},{24,8},{1,17},{9,25},{17,1},{25,9},{2,18},{10... | collective-permute-start | bytes 9437192 | tf_op jit(solution)/shard_map/ppermute | solution.py:146
  14.2 120.6 %collective-permute-start = (f32[128,5120]{1,0:T(8,128)}, f32[128,5120]{1,0:T(8,128)}, u32[]{:S(2)}, u32[]{:S(2)}) collective-permute-start(f32[128,5120]{1,0:T(8,128)} %slice.36), channel_id=1, source_target_pairs={{0,16},{8,24},{16,0},{24,8},{1,17},{9,25},{17,1},{25,9},{2,18},{10... | collective-permute-start | bytes 7864328 | tf_op jit(solution)/shard_map/ppermute | solution.py:146
  78.5 60.2 %collective-permute-start.3 = (f32[128,6144]{1,0:T(8,128)S(1)}, f32[128,6144]{1,0:T(8,128)}, u32[]{:S(2)}, u32[]{:S(2)}) collective-permute-start(f32[128,6144]{1,0:T(8,128)S(1)} %collective-permute-done.2), channel_id=1, source_target_pairs={{0,8},{8,0},{16,24},{24,16},{1,9},{9,1},{17,25},{25,17},{2,10},{10... | collective-permute-start | bytes 9437192 | tf_op jit(solution)/shard_map/ppermute | solution.py:152
  134.7 39.8 %collective-permute-start.6 = (f32[128,5120]{1,0:T(8,128)}, f32[128,5120]{1,0:T(8,128)S(1)}, u32[]{:S(2)}, u32[]{:S(2)}) collective-permute-start(f32[128,5120]{1,0:T(8,128)} %collective-permute-done), channel_id=1, source_target_pairs={{0,8},{8,0},{16,24},{24,16},{1,9},{9,1},{17,25},{25,17},{2,10},{10... | collective-permute-start | bytes 7864328 | tf_op jit(solution)/shard_map/ppermute | solution.py:152
  136.3 36.2 %collective-permute-start.5 = (f32[128,3072]{1,0:T(8,128)}, f32[128,3072]{1,0:T(8,128)S(1)}, u32[]{:S(2)}, u32[]{:S(2)}) collective-permute-start(f32[128,3072]{1,0:T(8,128)} %slice.37), channel_id=1, source_target_pairs={{0,16},{8,24},{16,0},{24,8},{1,17},{9,25},{17,1},{25,9},{2,18},{10... | collective-permute-start | bytes 4718600 | tf_op jit(solution)/shard_map/ppermute | solution.py:146
  172.4 10.6 %collective-permute-start.7 = (f32[128,3072]{1,0:T(8,128)S(1)}, f32[128,3072]{1,0:T(8,128)S(1)}, u32[]{:S(2)}, u32[]{:S(2)}) collective-permute-start(f32[128,3072]{1,0:T(8,128)S(1)} %collective-permute-done.5), channel_id=1, source_target_pairs={{0,8},{8,0},{16,24},{24,16},{1,9},{9,1},{17,25},{25,17},{2,10},{10... | collective-permute-start | bytes 4718600 | tf_op jit(solution)/shard_map/ppermute | solution.py:152
  173.3 24.7 %collective-permute-start.4 = (f32[128,2048]{1,0:T(8,128)S(1)}, f32[128,2048]{1,0:T(8,128)S(1)}, u32[]{:S(2)}, u32[]{:S(2)}) collective-permute-start(f32[128,2048]{1,0:T(8,128)S(1)} %slice.40), channel_id=1, source_target_pairs={{0,16},{8,24},{16,0},{24,8},{1,17},{9,25},{17,1},{25,9},{2,18},{10... | collective-permute-start | bytes 3145736 | tf_op jit(solution)/shard_map/ppermute | solution.py:146
  183.0 16.0 %copy-start.1 = (f32[256,512]{1,0:T(8,128)S(1)}, f32[256,512]{1,0:T(8,128)}, u32[]{:S(2)}) copy-start(f32[256,512]{1,0:T(8,128)} %fusion) | copy-start | bytes 1572868
  198.0 3.1 %collective-permute-start.8 = (f32[128,2048]{1,0:T(8,128)S(1)}, f32[128,2048]{1,0:T(8,128)S(1)}, u32[]{:S(2)}, u32[]{:S(2)}) collective-permute-start(f32[128,2048]{1,0:T(8,128)S(1)} %collective-permute-done.4), channel_id=1, source_target_pairs={{0,8},{8,0},{16,24},{24,16},{1,9},{9,1},{17,25},{25,17},{2,10},{10... | collective-permute-start | bytes 3145736 | tf_op jit(solution)/shard_map/ppermute | solution.py:152
  199.0 6.6 %copy-start = (f32[512,4096]{1,0:T(8,128)S(1)}, f32[512,4096]{1,0:T(8,128)}, u32[]{:S(2)}) copy-start(f32[512,4096]{1,0:T(8,128)} %all-gather.2.cloned.1.call-done.chol) | copy-start | bytes 25165828
Sparse Core Ops, SparseCore 0:
  9.5 122.2 all-gather.1

commit v3 on v2

--- a/solution.py
+++ b/solution.py
@@ -155,12 +155,25 @@
         return [terms(a, b, part(amplitudes, c)) for a, b in zip(pieces, crossed)]
 
     first, second = far(part(green_vectors, 0)), far(part(green_vectors, 1))
-    stacked = lax.all_gather(cholesky, "col", axis=0, tiled=True)
+    cols = lax.axis_size("col")
+    place = lax.axis_index("col")
+    pairing = [(i, i ^ 1) for i in range(cols)]
+    along = [
+        lax.ppermute(cholesky, "col", [(i, (i + hop) % cols) for i in range(cols)])
+        for hop in range(2, cols, 2)
+    ]
+    beside = [lax.ppermute(cholesky, "col", pairing)]
     near = lax.ppermute(green_vectors, "row", sibling)
     own = terms(green_vectors, near, amplitudes)
-    piece, own = lax.optimization_barrier((part(green_vectors, 2), own))
-    third = far(piece)
-    second, own = lax.optimization_barrier((second, own))
+    third = far(part(green_vectors, 2))
+    second, along, own = lax.optimization_barrier((second, along, own))
+    beside += [lax.ppermute(piece, "col", pairing) for piece in along]
+    deep = cholesky.shape[0]
+    stacked = jnp.zeros((cols * deep, cholesky.shape[1]), jnp.float32)
+    for at, both in enumerate(zip([cholesky] + along, beside)):
+        for side, piece in enumerate(both):
+            owner = lax.rem((place ^ side) - 2 * at + cols, cols)
+            stacked = lax.dynamic_update_slice(stacked, piece, (owner * deep, 0))
     sums = dots(first, cross(first), 0)
     piece, sums = lax.optimization_barrier((part(green_vectors, 3), sums))
     fourth = far(piece)

time: 255 us -> 284 us (1.11)
  local copies, waits for them, and re-layouts: 10.6 us -> 32.3 us
  waiting for transfers between devices: 129 us -> 148 us
  between operations: 13.5 us -> 0.14 us
    ppermute x0 -> x7, waiting for transfers between devices: none -> 43.1 us  [the longest x3 36 us: per_device(): beside += [lax.ppermute(piece, 'col', pairing) for piece in along]]
    ppermute x4, waiting for transfers between devices: 127 us -> 103 us  [far(): lax.ppermute(piece, 'row', [(i, (i + hop) % rows) for i in range(rows)])]
    dynamic_update_slice x0 -> x8, local copies, waits for them, and re-layouts: none -> 14.7 us  [per_device(): stacked = lax.dynamic_update_slice(stacked, piece, (owner * deep, 0))]
    broadcast_in_dim x0 -> x1, local copies, waits for them, and re-layouts: none -> 4.27 us  [per_device(): stacked = jnp.zeros((cols * deep, cholesky.shape[1]), jnp.float32)]
    ppermute x0 -> x7, starting transfers between devices: none -> 4.25 us  [the longest x3 2.48 us: per_device(): lax.ppermute(cholesky, 'col', [(i, (i + hop) % cols) for i in range(cols)])]
  transfers between devices with their start and end apart: 10 -> 16, of which waited for: 5 -> 7; matrix products, arithmetic and copies ran while one was open for 22% -> 27% of each run, Pallas kernels for 0% -> 0%
where the time goes in v3:
time: 284 us; the launch traced here: 283 us
  waiting for transfers between devices  148 us (52%)
  matrix products  49.7 us (18%)
  Pallas kernels  40.3 us (14%)
  local copies, waits for them, and re-layouts  32.3 us (11%)
  starting transfers between devices  12.3 us (4%)
    ppermute x4, waiting for transfers between devices, far(): lax.ppermute(piece, 'row', [(i, (i + hop) % rows) for i in range(rows)])  103 us
    dot_general x5, matrix products, three_pass(): lax.dot_general(left, right, (dims, ((), ())), precision=lax.Precision.HI...  49.7 us
    pallas_call x1, Pallas kernels, tail(): pl.pallas_call(functools.partial(tail_kernel, rows, cols), out_shape=jax....  40.3 us
    ppermute x3, waiting for transfers between devices, per_device(): beside += [lax.ppermute(piece, 'col', pairing) for piece in along]  36 us
    dynamic_update_slice x8, local copies, waits for them, and re-layouts, per_device(): stacked = lax.dynamic_update_slice(stacked, piece, (owner * deep, 0))  14.7 us
    slice x4, local copies, waits for them, and re-layouts, part(): return lax.slice_in_dim(array, cuts[c], cuts[c + 1], axis=1)  12.4 us
    ppermute x1, waiting for transfers between devices, per_device(): beside = [lax.ppermute(cholesky, 'col', pairing)]  7.1 us
  transfers between devices with their start and end apart: 16, of which 7 were waited for; matrix products, arithmetic and copies ran while one was open for 27% of the time, Pallas kernels for 0%

profile of v3, /device:TPU:13, one launch (start us, length us, event | category | flops | bytes accessed | tf_op | source)
XLA Modules:
  0.0 283.2 jit_solution(1451996199772188375)
XLA Ops:
  0.0 0.7 collective-permute-start.4
  0.7 3.8 %slice.40 = f32[128,6144]{1,0:T(8,128)} slice(f32[128,16384]{1,0:T(8,128)} %param.3), slice={[0:128], [0:6144]} | slice | bytes 6291456 | tf_op jit(solution)/shard_map/slice | solution.py:143
  4.5 1.2 collective-permute-start.5
  5.7 0.2 collective-permute-start.11
  6.0 1.3 collective-permute-start.1
  7.3 1.0 collective-permute-start.2
  8.3 3.5 %slice.36 = f32[128,5120]{1,0:T(8,128)} slice(f32[128,16384]{1,0:T(8,128)} %param.3), slice={[0:128], [6144:11264]} | slice | bytes 5242880 | tf_op jit(solution)/shard_map/slice | solution.py:143
  11.8 2.3 slice.39
  14.1 2.7 slice.42
  16.8 4.3 %broadcast_in_dim.7 = f32[512,4096]{1,0:T(8,128)} broadcast(f32[]{:T(128)} %constant.51.clone.1), dimensions={} | broadcast | bytes 8388612 | tf_op jit(solution)/shard_map/broadcast_in_dim | solution.py:172
  21.1 2.3 constant_dynamic-update-slice_fusion.7
  23.4 7.1 %collective-permute-done.11 = f32[64,4096]{1,0:T(8,128)} collective-permute-done((f32[64,4096]{1,0:T(8,128)}, f32[64,4096]{1,0:T(8,128)}, u32[]{:S(2)}, u32[]{:S(2)}) %collective-permute-start.11) | collective-permute-done | bytes 1048608 | tf_op jit(solution)/shard_map/ppermute | solution.py:165
  30.5 0.2 collective-permute-start.3
  30.6 43.7 %collective-permute-done.5 = f32[128,6144]{1,0:T(8,128)S(1)} collective-permute-done((f32[128,6144]{1,0:T(8,128)}, f32[128,6144]{1,0:T(8,128)S(1)}, u32[]{:S(2)}, u32[]{:S(2)}) %collective-permute-start.5) | collective-permute-done | bytes 3145760 | tf_op jit(solution)/shard_map/ppermute | solution.py:146
  74.4 0.9 collective-permute-start.6
  75.2 2.3 constant_dynamic-update-slice_fusion.6
  77.5 0.0 collective-permute-done.1
  77.5 1.2 collective-permute-start
  78.7 0.0 collective-permute-done.4
  78.7 0.3 collective-permute-start.8
  79.0 21.8 %fusion = f32[256,512]{1,0:T(8,128)} fusion(f32[512,16384]{1,0:T(8,128)} %param.4, f32[128,16384]{1,0:T(8,128)} %collective-permute-done.4, f32[128,16384]{1,0:T(8,128)} %param.3), kind=kOutput, calls=%fused_computation | convolution fusion | flops 12889096192 | bytes 50855936 | tf_op jit(solution)/shard_map/dot_general | solution.py:15
  100.8 0.0 copy-start.1
  100.8 0.0 collective-permute-done.2
  100.8 0.0 collective-permute-done.3
  100.8 35.5 %collective-permute-done = f32[128,5120]{1,0:T(8,128)} collective-permute-done((f32[128,5120]{1,0:T(8,128)}, f32[128,5120]{1,0:T(8,128)}, u32[]{:S(2)}, u32[]{:S(2)}) %collective-permute-start) | collective-permute-done | bytes 2621472 | tf_op jit(solution)/shard_map/ppermute | solution.py:146
  136.3 0.0 collective-permute-start.12
  136.3 0.0 collective-permute-done.6
  136.3 9.6 %fusion.4 = f32[256,512]{1,0:T(8,128)S(1)} fusion(f32[512,16384]{1,0:T(8,128)} %param.4, f32[128,6144]{1,0:T(8,128)} %collective-permute-done.6, f32[128,6144]{1,0:T(8,128)S(1)} %collective-permute-done.5), kind=kOutput, calls=%fused_computation.4 | convolution fusion | flops 4833411072 | bytes 19398656 | tf_op jit(solution)/shard_map/dot_general | solution.py:15
  145.9 24.1 %collective-permute-done.8 = f32[128,3072]{1,0:T(8,128)} collective-permute-done((f32[128,3072]{1,0:T(8,128)}, f32[128,3072]{1,0:T(8,128)}, u32[]{:S(2)}, u32[]{:S(2)}) %collective-permute-start.8) | collective-permute-done | bytes 1572896 | tf_op jit(solution)/shard_map/ppermute | solution.py:146
  170.0 0.9 collective-permute-start.10
  170.8 0.0 copy-done.1
  170.8 1.2 collective-permute-start.7
  172.0 0.3 collective-permute-start.13
  172.3 0.6 collective-permute-start.9
  172.9 2.3 constant_dynamic-update-slice_fusion.5
  175.1 0.0 collective-permute-done.12
  175.1 1.3 collective-permute-start.14
  176.4 1.1 constant_dynamic-update-slice_fusion.4
  177.6 2.3 constant_dynamic-update-slice_fusion.3
  179.8 16.8 %collective-permute-done.13 = f32[64,4096]{1,0:T(8,128)S(1)} collective-permute-done((f32[64,4096]{1,0:T(8,128)}, f32[64,4096]{1,0:T(8,128)S(1)}, u32[]{:S(2)}, u32[]{:S(2)}) %collective-permute-start.13) | collective-permute-done | bytes 1048608 | tf_op jit(solution)/shard_map/ppermute | solution.py:170
  196.7 1.1 constant_dynamic-update-slice_fusion.2
  197.8 2.3 constant_dynamic-update-slice_fusion.1
  200.0 19.1 %collective-permute-done.14 = f32[64,4096]{1,0:T(8,128)S(1)} collective-permute-done((f32[64,4096]{1,0:T(8,128)}, f32[64,4096]{1,0:T(8,128)S(1)}, u32[]{:S(2)}, u32[]{:S(2)}) %collective-permute-start.14) | collective-permute-done | bytes 1048608 | tf_op jit(solution)/shard_map/ppermute | solution.py:170
  219.2 1.1 constant_dynamic-update-slice_fusion.chol
  220.3 0.0 collective-permute-done.9
  220.3 8.4 %fusion.6 = f32[256,512]{1,0:T(8,128)S(1)} fusion(f32[512,16384]{1,0:T(8,128)} %param.4, f32[128,5120]{1,0:T(8,128)S(1)} %collective-permute-done.9, f32[128,5120]{1,0:T(8,128)} %collective-permute-done), kind=kOutput, calls=%fused_computation.6 | convolution fusion | flops 4027842560 | bytes 16252928 | tf_op jit(solution)/shard_map/dot_general | solution.py:15
  228.7 0.0 copy-start
  228.7 0.0 collective-permute-done.10
  228.7 5.9 %add_add_fusion = f32[256,512]{1,0:T(8,128)S(1)} fusion(f32[256,512]{1,0:T(8,128)S(1)} %fusion.4, f32[256,512]{1,0:T(8,128)S(1)} %fusion.6, f32[512,16384]{1,0:T(8,128)} %param.4, f32[128,3072]{1,0:T(8,128)S(1)} %collective-permute-done.10, f32[128,3072]{1,0:T(8,128)} %collective-permute-done.8), kind=kOutput, calls=%fused_computation.24 | convolution fusion | flops 2416967680 | bytes 11010048 | tf_op jit(solution)/shard_map/dot_general | solution.py:15
  234.5 0.0 collective-permute-done.7
  234.6 1.2 collective-permute-start.15
  235.8 0.1 broadcast_in_dim.6
  235.9 0.0 copy-done
  236.0 2.1 collective-permute-done.15
  238.1 4.0 %fusion.16 = f32[256,512]{1,0:T(8,128)S(1)} fusion(f32[512,16384]{1,0:T(8,128)} %param.4, f32[128,2048]{1,0:T(8,128)S(1)} %collective-permute-done.15, f32[128,2048]{1,0:T(8,128)S(1)} %collective-permute-done.7), kind=kOutput, calls=%fused_computation.16 | convolution fusion | flops 1611137024 | bytes 6815744 | tf_op jit(solution)/shard_map/dot_general | solution.py:15
  242.1 0.1 add.119
  242.2 40.3 %shard_map.37 = f32[64,1024]{1,0:T(8,128)S(1)} custom-call(f32[8,64,512]{2,1,0:T(8,128)S(1)} %bitcast.2, f32[512,4096]{1,0:T(8,128)} %constant_dynamic-update-slice_fusion.chol), custom_call_target="tpu_custom_call" | custom-call | tf_op jit(solution)/shard_map/pallas_call | solution.py:110
  282.5 0.7 copy.17
  (4 shorter events, 0.1 us)
Async XLA Ops:
  0.0 78.7 %collective-permute-start.4 = (f32[128,16384]{1,0:T(8,128)}, f32[128,16384]{1,0:T(8,128)}, u32[]{:S(2)}, u32[]{:S(2)}) collective-permute-start(f32[128,16384]{1,0:T(8,128)} %param.3), channel_id=1, source_target_pairs={{0,8},{8,0},{16,24},{24,16},{1,9},{9,1},{17,25},{25,17},{2,10},{10... | collective-permute-start | bytes 25165832 | tf_op jit(solution)/shard_map/ppermute | solution.py:166
  4.5 69.9 %collective-permute-start.5 = (f32[128,6144]{1,0:T(8,128)}, f32[128,6144]{1,0:T(8,128)S(1)}, u32[]{:S(2)}, u32[]{:S(2)}) collective-permute-start(f32[128,6144]{1,0:T(8,128)} %slice.40), channel_id=1, source_target_pairs={{0,16},{8,24},{16,0},{24,8},{1,17},{9,25},{17,1},{25,9},{2,18},{10... | collective-permute-start | bytes 9437192 | tf_op jit(solution)/shard_map/ppermute | solution.py:146
  5.7 24.7 %collective-permute-start.11 = (f32[64,4096]{1,0:T(8,128)}, f32[64,4096]{1,0:T(8,128)}, u32[]{:S(2)}, u32[]{:S(2)}) collective-permute-start(f32[64,4096]{1,0:T(8,128)} %param.5), channel_id=1, source_target_pairs={{0,1},{1,0},{2,3},{3,2},{4,5},{5,4},{6,7},{7,6},{8,9},{9,8},{10,11... | collective-permute-start | bytes 3145736 | tf_op jit(solution)/shard_map/ppermute | solution.py:165
  6.0 71.6 %collective-permute-start.1 = (f32[64,4096]{1,0:T(8,128)}, f32[64,4096]{1,0:T(8,128)}, u32[]{:S(2)}, u32[]{:S(2)}) collective-permute-start(f32[64,4096]{1,0:T(8,128)} %param.5), channel_id=1, source_target_pairs={{0,2},{1,3},{2,4},{3,5},{4,6},{5,7},{6,0},{7,1},{8,10},{9,11},{10,... | collective-permute-start | bytes 3145736 | tf_op jit(solution)/shard_map/ppermute | solution.py:162
  7.3 93.5 %collective-permute-start.2 = (f32[64,4096]{1,0:T(8,128)}, f32[64,4096]{1,0:T(8,128)}, u32[]{:S(2)}, u32[]{:S(2)}) collective-permute-start(f32[64,4096]{1,0:T(8,128)} %param.5), channel_id=1, source_target_pairs={{0,4},{1,5},{2,6},{3,7},{4,0},{5,1},{6,2},{7,3},{8,12},{9,13},{10,... | collective-permute-start | bytes 3145736 | tf_op jit(solution)/shard_map/ppermute | solution.py:162
  30.5 70.3 %collective-permute-start.3 = (f32[64,4096]{1,0:T(8,128)}, f32[64,4096]{1,0:T(8,128)}, u32[]{:S(2)}, u32[]{:S(2)}) collective-permute-start(f32[64,4096]{1,0:T(8,128)} %param.5), channel_id=1, source_target_pairs={{0,6},{1,7},{2,0},{3,1},{4,2},{5,3},{6,4},{7,5},{8,14},{9,15},{10,... | collective-permute-start | bytes 3145736 | tf_op jit(solution)/shard_map/ppermute | solution.py:162
  74.4 61.9 %collective-permute-start.6 = (f32[128,6144]{1,0:T(8,128)S(1)}, f32[128,6144]{1,0:T(8,128)}, u32[]{:S(2)}, u32[]{:S(2)}) collective-permute-start(f32[128,6144]{1,0:T(8,128)S(1)} %collective-permute-done.5), channel_id=1, source_target_pairs={{0,8},{8,0},{16,24},{24,16},{1,9},{9,1},{17,25},{25,17},{2,10},{10... | collective-permute-start | bytes 9437192 | tf_op jit(solution)/shard_map/ppermute | solution.py:152
  77.5 58.7 %collective-permute-start = (f32[128,5120]{1,0:T(8,128)}, f32[128,5120]{1,0:T(8,128)}, u32[]{:S(2)}, u32[]{:S(2)}) collective-permute-start(f32[128,5120]{1,0:T(8,128)} %slice.36), channel_id=1, source_target_pairs={{0,16},{8,24},{16,0},{24,8},{1,17},{9,25},{17,1},{25,9},{2,18},{10... | collective-permute-start | bytes 7864328 | tf_op jit(solution)/shard_map/ppermute | solution.py:146
  78.7 91.2 %collective-permute-start.8 = (f32[128,3072]{1,0:T(8,128)}, f32[128,3072]{1,0:T(8,128)}, u32[]{:S(2)}, u32[]{:S(2)}) collective-permute-start(f32[128,3072]{1,0:T(8,128)} %slice.42), channel_id=1, source_target_pairs={{0,16},{8,24},{16,0},{24,8},{1,17},{9,25},{17,1},{25,9},{2,18},{10... | collective-permute-start | bytes 4718600 | tf_op jit(solution)/shard_map/ppermute | solution.py:146
  100.8 70.0 %copy-start.1 = (f32[128,2048]{1,0:T(8,128)S(1)}, f32[128,2048]{1,0:T(8,128)}, u32[]{:S(2)}) copy-start(f32[128,2048]{1,0:T(8,128)} %slice.39) | copy-start | bytes 3145732
  136.3 38.9 %collective-permute-start.12 = (f32[64,4096]{1,0:T(8,128)}, f32[64,4096]{1,0:T(8,128)S(1)}, u32[]{:S(2)}, u32[]{:S(2)}) collective-permute-start(f32[64,4096]{1,0:T(8,128)} %collective-permute-done.1), channel_id=1, source_target_pairs={{0,1},{1,0},{2,3},{3,2},{4,5},{5,4},{6,7},{7,6},{8,9},{9,8},{10,11... | collective-permute-start | bytes 3145736 | tf_op jit(solution)/shard_map/ppermute | solution.py:170
  170.0 58.7 %collective-permute-start.10 = (f32[128,3072]{1,0:T(8,128)}, f32[128,3072]{1,0:T(8,128)S(1)}, u32[]{:S(2)}, u32[]{:S(2)}) collective-permute-start(f32[128,3072]{1,0:T(8,128)} %collective-permute-done.8), channel_id=1, source_target_pairs={{0,8},{8,0},{16,24},{24,16},{1,9},{9,1},{17,25},{25,17},{2,10},{10... | collective-permute-start | bytes 4718600 | tf_op jit(solution)/shard_map/ppermute | solution.py:152
  170.8 63.7 %collective-permute-start.7 = (f32[128,2048]{1,0:T(8,128)S(1)}, f32[128,2048]{1,0:T(8,128)S(1)}, u32[]{:S(2)}, u32[]{:S(2)}) collective-permute-start(f32[128,2048]{1,0:T(8,128)S(1)} %copy-done.1), channel_id=1, source_target_pairs={{0,16},{8,24},{16,0},{24,8},{1,17},{9,25},{17,1},{25,9},{2,18},{10... | collective-permute-start | bytes 3145736 | tf_op jit(solution)/shard_map/ppermute | solution.py:146
  172.0 24.6 %collective-permute-start.13 = (f32[64,4096]{1,0:T(8,128)}, f32[64,4096]{1,0:T(8,128)S(1)}, u32[]{:S(2)}, u32[]{:S(2)}) collective-permute-start(f32[64,4096]{1,0:T(8,128)} %collective-permute-done.2), channel_id=1, source_target_pairs={{0,1},{1,0},{2,3},{3,2},{4,5},{5,4},{6,7},{7,6},{8,9},{9,8},{10,11... | collective-permute-start | bytes 3145736 | tf_op jit(solution)/shard_map/ppermute | solution.py:170
  172.3 48.0 %collective-permute-start.9 = (f32[128,5120]{1,0:T(8,128)}, f32[128,5120]{1,0:T(8,128)S(1)}, u32[]{:S(2)}, u32[]{:S(2)}) collective-permute-start(f32[128,5120]{1,0:T(8,128)} %collective-permute-done), channel_id=1, source_target_pairs={{0,8},{8,0},{16,24},{24,16},{1,9},{9,1},{17,25},{25,17},{2,10},{10... | collective-permute-start | bytes 7864328 | tf_op jit(solution)/shard_map/ppermute | solution.py:152
  175.1 44.0 %collective-permute-start.14 = (f32[64,4096]{1,0:T(8,128)}, f32[64,4096]{1,0:T(8,128)S(1)}, u32[]{:S(2)}, u32[]{:S(2)}) collective-permute-start(f32[64,4096]{1,0:T(8,128)} %collective-permute-done.3), channel_id=1, source_target_pairs={{0,1},{1,0},{2,3},{3,2},{4,5},{5,4},{6,7},{7,6},{8,9},{9,8},{10,11... | collective-permute-start | bytes 3145736 | tf_op jit(solution)/shard_map/ppermute | solution.py:170
  228.7 7.2 %copy-start = (f32[256,512]{1,0:T(8,128)S(1)}, f32[256,512]{1,0:T(8,128)}, u32[]{:S(2)}) copy-start(f32[256,512]{1,0:T(8,128)} %fusion) | copy-start | bytes 1572868
  234.6 3.5 %collective-permute-start.15 = (f32[128,2048]{1,0:T(8,128)S(1)}, f32[128,2048]{1,0:T(8,128)S(1)}, u32[]{:S(2)}, u32[]{:S(2)}) collective-permute-start(f32[128,2048]{1,0:T(8,128)S(1)} %collective-permute-done.7), channel_id=1, source_target_pairs={{0,8},{8,0},{16,24},{24,16},{1,9},{9,1},{17,25},{25,17},{2,10},{10... | collective-permute-start | bytes 3145736 | tf_op jit(solution)/shard_map/ppermute | solution.py:152
